TPU v7x, 128 devices: a whole 4x4x4 slice. The times are simulated.
128 devices in a mesh: gx: 8 (over y, core), gy: 16 (over z, x).
Axes of the slice: x: 4, y: 4, z: 4, core: 2. Of those that a mesh axis runs over, the one named last changes fastest.
Arguments:
- beta: float32 [16, 64, 2048], P(None, 'gx', 'gy'), may hold values from -6 to 6
- design: float32 [16, 16], replicated, may hold values from -1.5 to 1.5
- prior: float32 [16], replicated, may hold values from 0.25 to 4
- kept: int32 [16, 64, 2048], P(None, 'gx', 'gy'), may hold values from 1 to 40
- removed: int32 [16, 64, 2048], P(None, 'gx', 'gy'), may hold values from 0 to 8
- removed_labels: int32 [16, 64, 2048], P(None, 'gx', 'gy'), may hold values from 0 to 8, as said below
Outputs:
- newton_step: float32 [16, 64, 2048], P(None, 'gx', 'gy')
Inputs may be any that keep to these rules, and one draw needn't show every extreme that they name: `removed_labels`: each entry is at most the entry of removed at the same place.
All inputs are finite; a program needn't handle non-finite values.
Results may differ from a plain program's by a relative error of at most 0.00022.
Values sent between devices are 32-bit elements; how exact they have to be, the bound alone decides.
A program may use at most 64 MiB of HBM per device.

v0:
```python
import jax
import jax.numpy as jnp
from jax import lax
from jax.sharding import PartitionSpec as P

ITERS = 4
SWEEPS = 2
LEVELS = 4
COARSE_SWEEPS = 4


damping = 0.7
highest = lax.Precision.HIGHEST


def extended(block, sides, width):
    for axis, dim in sides:
        count = lax.axis_size(axis)
        forward = [(i, i + 1) for i in range(count - 1)]
        backward = [(target, source) for source, target in forward]
        low = lax.ppermute(
            lax.slice_in_dim(block, block.shape[dim] - width, None, axis=dim), axis, forward
        )
        high = lax.ppermute(lax.slice_in_dim(block, 0, width, axis=dim), axis, backward)
        block = jnp.concatenate([low, block, high], axis=dim)
    return block


def gauss_jordan(blocks):
    size = blocks.shape[0]
    for pivot_at in range(size):
        pivots = blocks[pivot_at, pivot_at]
        scaled = blocks[pivot_at].at[pivot_at].set(1.0) / pivots[None]
        factors = blocks[:, pivot_at]
        blocks = blocks.at[:, pivot_at].set(0.0) - factors[:, None] * scaled[None]
        blocks = blocks.at[pivot_at].set(scaled)
    return blocks


def apply_inverse(inverse, vector):
    return jnp.einsum("klxy,lxy->kxy", inverse, vector, precision=highest)


def operate(field, padded, design, weights, prior, scale):
    inner = jnp.einsum("jk,kxy->jxy", design, field, precision=highest)
    data_term = jnp.einsum("jk,jxy->kxy", design, weights * inner, precision=highest)
    beside = padded[:, 2:, 1:-1] + padded[:, :-2, 1:-1] + padded[:, 1:-1, 2:] + padded[:, 1:-1, :-2]
    return data_term + scale * prior[:, None, None] * (4.0 * field - beside)


def restrict(field):
    chans, rows, cols = field.shape
    return field.reshape(chans, rows // 2, 2, cols // 2, 2).sum(axis=(2, 4))


def prolong(field):
    return jnp.repeat(jnp.repeat(field, 2, axis=1), 2, axis=2)


def build_inverse(design, weights, prior, scale):
    outer = design[:, :, None] * design[:, None, :]
    blocks = jnp.einsum("jkl,jxy->klxy", outer, weights, precision=highest)
    blocks = blocks + (4.0 * scale * jnp.diag(prior))[:, :, None, None]
    return gauss_jordan(blocks)


def fine_pad(field):
    return extended(field, (("gx", 1), ("gy", 2)), 1)


def coarse_pad(field):
    return extended(field, (("gx", 1), ("gy", 2)), 1)


def smooth(field, rhs, padder, design, weights, inverse, prior, scale):
    leftover = rhs - operate(field, padder(field), design, weights, prior, scale)
    return field + damping * apply_inverse(inverse, leftover)


def sweeps(rhs, count, padder, design, weights, inverse, prior, scale):
    field = damping * apply_inverse(inverse, rhs)
    for sweep in range(count - 1):
        field = smooth(field, rhs, padder, design, weights, inverse, prior, scale)
    return field


def multigrid(rhs, level, tables, design, prior):
    weights, inverse = tables[level]
    scale = 2.0**level
    if level == len(tables) - 1:
        return sweeps(rhs, COARSE_SWEEPS, coarse_pad, design, weights, inverse, prior, scale)
    field = sweeps(rhs, SWEEPS, fine_pad, design, weights, inverse, prior, scale)
    leftover = rhs - operate(field, fine_pad(field), design, weights, prior, scale)
    field = field + prolong(multigrid(restrict(leftover), level + 1, tables, design, prior))
    for sweep in range(SWEEPS):
        field = smooth(field, rhs, fine_pad, design, weights, inverse, prior, scale)
    return field


def residual_product(residual, precond):
    return lax.psum(jnp.sum(residual * precond), ("gx", "gy"))


def local(beta, design, prior, kept, removed, removed_labels):
    logits = jnp.einsum("jk,kxy->jxy", design, beta, precision=highest)
    prob = 1.0 / (1.0 + jnp.exp(-logits))
    weights = kept.astype(jnp.float32) * prob * (1.0 - prob)
    source = removed.astype(jnp.float32) * prob - removed_labels.astype(jnp.float32)
    rhs = jnp.einsum("jk,jxy->kxy", design, source, precision=highest)
    tables = []
    for level in range(LEVELS):
        if level > 0:
            weights = restrict(weights)
        tables.append((weights, build_inverse(design, weights, prior, 2.0**level)))
    fine_weights = tables[0][0]

    def precondition(residual):
        return multigrid(residual, 0, tables, design, prior)

    newton_step = jnp.zeros_like(rhs)
    residual = rhs
    precond = precondition(residual)
    direction = precond
    gamma = residual_product(residual, precond)
    for step in range(ITERS):
        image = operate(direction, fine_pad(direction), design, fine_weights, prior, 1.0)
        alpha = gamma / lax.psum(jnp.sum(direction * image), ("gx", "gy"))
        newton_step = newton_step + alpha * direction
        residual = residual - alpha * image
        if step + 1 < ITERS:
            precond = precondition(residual)
            gamma_next = residual_product(residual, precond)
            direction = precond + gamma_next / gamma * direction
            gamma = gamma_next
    return newton_step


def solution(mesh):
    placed = (
        P(None, "gx", "gy"),
        P(),
        P(),
        P(None, "gx", "gy"),
        P(None, "gx", "gy"),
        P(None, "gx", "gy"),
    )
    return jax.shard_map(
        local, mesh=mesh, in_specs=placed, out_specs=P(None, "gx", "gy"), check_vma=False
    )
```

profile of v0, /device:TPU:1, one launch (start us, length us, event | category | flops | bytes accessed | tf_op | source)
XLA Modules:
  0.0 1821.1 jit_solution(732086197900430185)
XLA Ops:
  321.5 6.7 collective-permute-start.23
  338.9 6.7 collective-permute-start.27
  355.8 6.7 collective-permute-start.31
  372.6 6.7 collective-permute-start.35
  389.7 6.7 collective-permute-start.39
  406.8 6.6 collective-permute-start.43
  424.1 6.6 collective-permute-start.47
  441.4 6.6 collective-permute-start.51
  459.3 6.7 collective-permute-start.55
  477.1 7.1 collective-permute-start.59
  495.0 6.7 collective-permute-start.63
  504.0 79.6 %all-reduce = (f32[]{:T(128)}, f32[]{:T(128)}) all-reduce(f32[]{:T(128)} %get-tuple-element.2310, f32[]{:T(128)} %get-tuple-element.2309), channel_id=1, replica_groups=mesh['gx'=8,'gy'=16] {'gx','gy'}, use_global_device_ids=true, to_apply=%region_11.12 | all-reduce | flops 2 | bytes 16 | tf_op jit(solution)/shard_map/psum | solution.py:101
  670.7 6.2 collective-permute-start.87
  687.5 6.7 collective-permute-start.91
  704.4 6.7 collective-permute-start.95
  721.2 6.7 collective-permute-start.99
  738.3 6.7 collective-permute-start.103
  755.4 6.6 collective-permute-start.107
  772.7 6.6 collective-permute-start.111
  790.0 6.6 collective-permute-start.115
  807.8 6.7 collective-permute-start.119
  825.7 6.9 collective-permute-start.123
  835.0 76.7 %psum.58 = f32[]{:T(128)} all-reduce(f32[]{:T(128)} %multiply_reduce_fusion.52), channel_id=1, replica_groups=mesh['gx'=8,'gy'=16] {'gx','gy'}, use_global_device_ids=true, to_apply=%region_19.20 | all-reduce | flops 1 | bytes 8 | tf_op jit(solution)/shard_map/psum | solution.py:101
  927.4 67.7 %psum.59 = f32[]{:T(128)} all-reduce(f32[]{:T(128)} %get-tuple-element.2556), channel_id=1, replica_groups=mesh['gx'=8,'gy'=16] {'gx','gy'}, use_global_device_ids=true, to_apply=%region_21.22 | all-reduce | flops 1 | bytes 8 | tf_op jit(solution)/shard_map/psum | solution.py:127
  1082.1 6.6 collective-permute-start.151
  1099.3 6.7 collective-permute-start.155
  1116.2 6.7 collective-permute-start.159
  1133.1 6.7 collective-permute-start.163
  1150.1 6.7 collective-permute-start.167
  1167.2 6.6 collective-permute-start.171
  1184.6 6.6 collective-permute-start.175
  1201.9 6.9 collective-permute-start.179
  1219.7 6.7 collective-permute-start.183
  1237.5 6.7 collective-permute-start.187
  1246.8 76.5 %psum.60 = f32[]{:T(128)} all-reduce(f32[]{:T(128)} %multiply_reduce_fusion.50), channel_id=1, replica_groups=mesh['gx'=8,'gy'=16] {'gx','gy'}, use_global_device_ids=true, to_apply=%region_27.28 | all-reduce | flops 1 | bytes 8 | tf_op jit(solution)/shard_map/psum | solution.py:101
  1339.0 67.8 %psum.61 = f32[]{:T(128)} all-reduce(f32[]{:T(128)} %get-tuple-element.2558), channel_id=1, replica_groups=mesh['gx'=8,'gy'=16] {'gx','gy'}, use_global_device_ids=true, to_apply=%region_29.30 | all-reduce | flops 1 | bytes 8 | tf_op jit(solution)/shard_map/psum | solution.py:127
  1493.8 6.4 collective-permute-start.215
  1510.8 6.7 collective-permute-start.219
  1527.7 6.7 collective-permute-start.223
  1544.6 6.7 collective-permute-start.227
  1561.6 6.7 collective-permute-start.231
  1578.7 6.9 collective-permute-start.235
  1596.3 6.6 collective-permute-start.239
  1613.6 6.6 collective-permute-start.243
  1631.4 6.7 collective-permute-start.247
  1649.3 6.7 collective-permute-start.251
  1658.6 76.5 %psum.62 = f32[]{:T(128)} all-reduce(f32[]{:T(128)} %multiply_reduce_fusion.48), channel_id=1, replica_groups=mesh['gx'=8,'gy'=16] {'gx','gy'}, use_global_device_ids=true, to_apply=%region_35.36 | all-reduce | flops 1 | bytes 8 | tf_op jit(solution)/shard_map/psum | solution.py:101
  1750.7 67.9 %psum.63 = f32[]{:T(128)} all-reduce(f32[]{:T(128)} %fusion.74), channel_id=1, replica_groups=mesh['gx'=8,'gy'=16] {'gx','gy'}, use_global_device_ids=true, to_apply=%region_37.38 | all-reduce | flops 1 | bytes 8 | tf_op jit(solution)/shard_map/psum | solution.py:127
  (1546 shorter events, 1018.2 us)
Async XLA Ops:
  84.8 157.1 %collective-permute-start = (f32[16,1,128]{2,0,1:T(8,128)S(1)}, f32[16,1,128]{2,0,1:T(8,128)S(1)}, u32[]{:S(2)}, u32[]{:S(2)}) collective-permute-start(f32[16,1,128]{2,0,1:T(8,128)S(1)} %get-tuple-element.2394), channel_id=1, source_target_pairs={{16,0},{32,16},{48,32},{64,48},{80,64},{96,80},{112,96},{17,1},{33... | collective-permute-start | bytes 24584 | tf_op jit(solution)/shard_map/ppermute | solution.py:24
  88.1 153.8 %collective-permute-start.1 = (f32[16,1,128]{2,0,1:T(8,128)S(1)}, f32[16,1,128]{2,0,1:T(8,128)S(1)}, u32[]{:S(2)}, u32[]{:S(2)}) collective-permute-start(f32[16,1,128]{2,0,1:T(8,128)S(1)} %get-tuple-element.2393), channel_id=1, source_target_pairs={{0,16},{16,32},{32,48},{48,64},{64,80},{80,96},{96,112},{1,17},{17... | collective-permute-start | bytes 24584 | tf_op jit(solution)/shard_map/ppermute | solution.py:21
  320.2 8.2 collective-permute-start.22
  337.6 8.1 collective-permute-start.26
  354.5 8.1 collective-permute-start.30
  371.4 8.1 collective-permute-start.34
  388.4 8.1 collective-permute-start.38
  405.5 8.1 collective-permute-start.42
  422.8 8.1 collective-permute-start.46
  440.1 8.1 collective-permute-start.50
  458.0 8.2 collective-permute-start.54
  459.3 8.2 collective-permute-start.55
  475.8 8.6 collective-permute-start.58
  477.1 8.2 collective-permute-start.59
  493.7 8.2 collective-permute-start.62
  495.0 8.2 collective-permute-start.63
  686.2 8.1 collective-permute-start.90
  703.1 8.1 collective-permute-start.94
  720.0 8.1 collective-permute-start.98
  737.0 8.1 collective-permute-start.102
  754.1 8.1 collective-permute-start.106
  771.4 8.1 collective-permute-start.110
  788.7 8.1 collective-permute-start.114
  806.5 8.2 collective-permute-start.118
  807.8 8.2 collective-permute-start.119
  824.4 8.4 collective-permute-start.122
  825.7 8.2 collective-permute-start.123
  1098.0 8.1 collective-permute-start.154
  1114.9 8.2 collective-permute-start.158
  1131.8 8.1 collective-permute-start.162
  1148.8 8.1 collective-permute-start.166
  1183.3 8.1 collective-permute-start.174
  1200.6 8.3 collective-permute-start.178
  1218.4 8.2 collective-permute-start.182
  1219.7 8.2 collective-permute-start.183
  1236.2 8.2 collective-permute-start.186
  1237.5 8.2 collective-permute-start.187
  1509.5 8.1 collective-permute-start.218
  1526.4 8.2 collective-permute-start.222
  1543.3 8.1 collective-permute-start.226
  1560.3 8.1 collective-permute-start.230
  1577.5 8.3 collective-permute-start.234
  1595.0 8.1 collective-permute-start.238
  1612.3 8.1 collective-permute-start.242
  1630.1 8.2 collective-permute-start.246
  1631.4 8.2 collective-permute-start.247
  1648.0 8.2 collective-permute-start.250
  1649.3 8.2 collective-permute-start.251
  (214 other events, 1341.3 us)
where the time goes:
time: 1850 us; the launch traced here: 1820 us
  starting transfers between devices  894 us (48%)
  blocking collectives  513 us (28%)
  local copies, waits for them, and re-layouts  149 us (8%)
  waiting for transfers between devices  111 us (6%)
  other arithmetic  104 us (6%)
  matrix products  33.5 us (2%)
    ppermute x128, starting transfers between devices, extended(): lax.ppermute(lax.slice_in_dim(block, block.shape[dim] - width, None, axis...  679 us
    psum x4, blocking collectives, residual_product(): return lax.psum(jnp.sum(residual * precond), ('gx', 'gy'))  309 us
    ppermute x128, starting transfers between devices, extended(): lax.ppermute(lax.slice_in_dim(block, 0, width, axis=dim), axis, backward)  215 us
    psum x3, blocking collectives, local(): alpha = gamma / lax.psum(jnp.sum(direction * image), ('gx', 'gy'))  203 us
    ppermute x128, waiting for transfers between devices, extended(): lax.ppermute(lax.slice_in_dim(block, block.shape[dim] - width, None, axis...  106 us
    scatter x64, local copies, waits for them, and re-layouts, gauss_jordan(): scaled = blocks[pivot_at].at[pivot_at].set(1.0) / pivots[None]  75.5 us
    scatter x64, other arithmetic, gauss_jordan(): blocks = blocks.at[pivot_at].set(scaled)  42.9 us
  transfers between devices with their start and end apart: 256, of which 134 were waited for; matrix products, arithmetic and copies ran while one was open for 9% of the time, Pallas kernels for 0%

commit v1 on v0

v1 whole, which is shorter than its diff:
```python
import jax
import jax.numpy as jnp
from jax import lax
from jax.experimental import pallas as pl
from jax.experimental.pallas import tpu as pltpu
from jax.sharding import PartitionSpec as P

K = 16
ITERS = 4
NTILES = 7
GX, GY = 8, 16
damping = 0.7
keep = 1.0 - damping
MESH = pl.DeviceIdType.MESH
F32 = jnp.float32

level_tiles = {0: (0, 1, 2), 1: (3, 4), 2: (5,), 3: (6,)}
tile_level = (0, 0, 0, 1, 1, 2, 3)
around = ((-1, -1), (-1, 0), (-1, 1), (0, -1), (0, 1), (1, -1), (1, 0), (1, 1))
sideways = tuple(o for o in around if o[1] != 0)


def iota(axis):
    return lax.broadcasted_iota(jnp.int32, (8, 128), axis)


def take(x, index, axis):
    return jnp.take_along_axis(x, index, axis=axis, mode="promise_in_bounds")


def lroll(x, shift):
    return pltpu.roll(x, shift % 128, x.ndim - 1)


def sroll(x, shift):
    return pltpu.roll(x, shift % 8, x.ndim - 2)


def body(
    beta, design, prior, kept, removed, labels, out,
    dv, pv, mask, nat, wt, a, mi, mb,
    fb, d1, d2, rho, v,
    zs, qs, ss, ds, xs, rs, us, ws, scal,
    tw, tf, pw, pf, psw, psf, g1b, g2b, s1w, s1f, s2w, s2f, r1w, r1f, r2w, r2f,
    lsend, lgx, lgy, lsum,
    e0s, e0r, e1s, e1r, e2s, e2r, ags, agr, bgs, bgr,
):
    mx, my = lax.axis_index("gx"), lax.axis_index("gy")
    sub, lane = iota(0), iota(1)

    def device(dx, dy):
        return (lax.rem(mx + dx + GX, GX), lax.rem(my + dy + GY, GY))

    barrier = pltpu.get_barrier_semaphore()
    peers = [(d, 0) for d in range(1, GX)] + [(0, d) for d in range(1, GY)]
    peers += [o for o in around if o[0] != 0 and o[1] != 0]
    for dx, dy in peers:
        pl.semaphore_signal(barrier, inc=1, device_id=device(dx, dy), device_id_type=MESH)

    def remote(src, dst, ssem, rsem, dx, dy):
        return pltpu.make_async_remote_copy(
            src_ref=src, dst_ref=dst, send_sem=ssem, recv_sem=rsem, device_id=device(dx, dy), device_id_type=MESH
        )

    def copies0(t, p, ps, k):
        out = [
            remote(t.at[pl.ds(0, 64)], t.at[pl.ds(128, 64)], e0s.at[k, 0], e0r.at[k, 0], -1, 0),
            remote(t.at[pl.ds(64, 64)], t.at[pl.ds(192, 64)], e0s.at[k, 1], e0r.at[k, 1], 1, 0),
        ]
        for j, (dx, dy) in enumerate(sideways):
            slot = sideways.index((-dx, -dy))
            out.append(remote(ps, p.at[slot], e0s.at[k, 2 + j], e0r.at[k, 2 + j], dx, dy))
        return out

    group = (lane + 4) // 8 % 16
    right_side = lane % 8 < 4
    even_half = (lane < 32) | (lane >= 96)

    def pack(rows_of, ps):
        total = jnp.zeros((8, 128), F32)
        for c in range(K):
            x = rows_of(c)
            total = jnp.where(group == c, lroll(x, 8 * c), total)
        ps[...] = total

    def load0(t, p, dst):
        def merged(dx):
            return jnp.where(right_side, p[sideways.index((dx, 1))], p[sideways.index((dx, -1))])

        here, below, above = merged(0), merged(1), merged(-1)
        even = jnp.where(sub < 4, here, sroll(jnp.where(sub < 2, below, above), 4))
        odd = jnp.where(sub < 4, sroll(here, 4), jnp.where(sub < 6, below, above))
        for c in range(K):
            dst[0, pl.ds(8 * c, 8), :] = t[pl.ds(c, 8, stride=32), :]
            dst[1, pl.ds(8 * c, 8), :] = t[pl.ds(16 + c, 8, stride=32), :]
            dst[2, pl.ds(8 * c, 8), :] = jnp.where(even_half, lroll(even, -8 * c), lroll(odd, 64 - 8 * c))

    def natural_start(src, t, p, ps, k):
        for r in range(8):
            t[pl.ds(16 * r, 16), :] = src[pl.ds(r, 16, stride=8), :]
        pack(lambda c: jnp.concatenate([src[pl.ds(8 * c + i, 4, stride=2), :] for i in range(2)], axis=0), ps)
        for copy in copies0(t, p, ps, k):
            copy.start()

    lane_even = lane % 2 == 0
    split = jnp.where(lane < 64, 2 * lane, 2 * (lane - 64) + 1)

    def restrict_pairs(src, first, g):
        for c in range(8):
            lo = src[first, pl.ds(8 * c, 8), :] + src[first + 1, pl.ds(8 * c, 8), :]
            hi = src[first, pl.ds(8 * c + 64, 8), :] + src[first + 1, pl.ds(8 * c + 64, 8), :]
            g[pl.ds(8 * c, 8), :] = take(jnp.where(lane_even, lo + lroll(lo, -1), hi + lroll(hi, 1)), split, 1)

    def copies1(s, r, k):
        rows = {1: (0, 40, 88), -1: (8, 40, 32), 0: (8, 32, 0)}
        out = []
        for j, (dx, dy) in enumerate(around):
            start, size, target = rows[dx]
            out.append(
                remote(s.at[pl.ds(start, size)], r.at[1 - dy, pl.ds(target, size)], e1s.at[k, j], e1r.at[k, j], dx, dy)
            )
        return out

    def start1(src, s, r, k):
        restrict_pairs(src, 0, g1b)
        s[pl.ds(0, 8), :] = g1b[pl.ds(7, 8, stride=8), :]
        for i in range(5):
            s[pl.ds(8 + 8 * i, 8), :] = g1b[pl.ds(i, 8, stride=8), :]
        for copy in copies1(s, r, k):
            copy.start()
        r[1, pl.ds(0, 32), :] = s[pl.ds(8, 32), :]

    middle = (lane >= 32) & (lane < 96)
    from_left = (lane // 32) % 2 == 1

    def load1(r, dst):
        for tile, base in ((3, 0), (4, 8)):
            for c in range(8):
                left, here, right = (r[g, pl.ds(base + c, 8, stride=16), :] for g in range(3))
                side = jnp.where(from_left, left, right)
                dst[tile, pl.ds(8 * c, 8), :] = jnp.where(middle, lroll(here, 32), lroll(side, 96))
                dst[tile, pl.ds(8 * c + 64, 8), :] = jnp.where(middle, lroll(here, 96), lroll(side, 32))

    def copies2(s, r, k):
        return [
            remote(s, r.at[pl.ds(16 * (GX - d), 16)], e2s.at[k, d - 1], e2r.at[k, d - 1], d, 0) for d in range(1, GX)
        ]

    def start2(src, s, r, k):
        restrict_pairs(src, 3, g2b)
        s[pl.ds(0, 8), :] = g2b[pl.ds(0, 8, stride=8), :]
        s[pl.ds(8, 8), :] = g2b[pl.ds(1, 8, stride=8), :]
        for copy in copies2(s, r, k):
            copy.start()
        r[pl.ds(0, 16), :] = s[...]

    def load2(r, dst):
        for c in range(8):
            even, odd = r[pl.ds(c, 8, stride=16), :], r[pl.ds(8 + c, 8, stride=16), :]
            dst[5, pl.ds(8 * c, 8), :] = jnp.where(lane < 64, even, lroll(odd, 64))
            dst[5, pl.ds(8 * c + 64, 8), :] = jnp.where(lane < 64, lroll(even, 64), odd)

    def finish(copies):
        for copy in copies:
            copy.wait_recv()
        for copy in copies:
            copy.wait_send()

    twice = 2 * lane % 64

    def restrict3(src, dst):
        for c in range(K):
            x = src[5, pl.ds(8 * c, 8), :]
            x = x + lroll(x, 64)
            dst[6, pl.ds(8 * c, 8), :] = take(x + lroll(x, -1), twice, 1)

    def fill(j, carry):
        for k in range(K):
            dv[j, k] = jnp.full((8, 128), design[j, k], F32)
        return carry

    lax.fori_loop(0, K, fill, 0)
    for t in range(NTILES):
        for k in range(K):
            pv[t, pl.ds(8 * k, 8), :] = jnp.full((8, 128), prior[k] * 2.0 ** tile_level[t], F32)

    def one(condition):
        return jnp.where(condition, 1.0, 0.0).astype(F32)

    for t in range(2):
        row = jnp.where(sub < 6, 2 * sub, 2 * sub - 16) + t
        at = 8 * mx + row
        mask[t] = one((at >= 0) & (at < 64))
    row = jnp.where(sub < 6, 2 * sub, 2 * sub - 16) + jnp.where(even_half, 0, 1)
    at = 8 * mx + row
    offset = (lane + 32) % 64 - 32
    column = 128 * my + jnp.where(offset < 0, offset, 128 + offset)
    mask[2] = one((at >= 0) & (at < 64) & (offset >= -4) & (offset < 4) & (column >= 0) & (column < 2048))
    for t in range(2):
        row = jnp.where(sub < 5, 2 * sub, 2 * sub - 16) + t
        at = 4 * mx + row
        column = lane - 32
        near = (row >= -5) & (row <= 8) & (column >= -26) & (column < 90)
        column = 64 * my + column
        mask[3 + t] = one(near & (at >= 0) & (at < 32) & (column >= 0) & (column < 1024))
    column = lane % 64 - 16
    near = (column >= -12) & (column < 44)
    column = 32 * my + column
    mask[5] = one(near & (column >= 0) & (column < 512))
    column = lane - 8
    near = (column >= -5) & (column < 21)
    column = 16 * my + column
    mask[6] = one(near & (column >= 0) & (column < 256))
    at = lax.rem(mx + sub, GX)
    first, last = at == 0, at == GX - 1
    mask[7] = one(~(((lane < 64) & first) | ((lane >= 64) & last)))
    mask[8] = one(~first)
    mask[9] = one(~last)

    logits = dv[:, 0] * beta[0]
    for k in range(1, K):
        logits = logits + dv[:, k] * beta[k]
    prob = 1.0 / (1.0 + jnp.exp(-logits))
    nat[0] = (kept[...].astype(F32) * prob * (1.0 - prob)).reshape(128, 128)
    nat[1] = (removed[...].astype(F32) * prob - labels[...].astype(F32)).reshape(128, 128)
    total = dv[0] * nat[1, pl.ds(0, 8), :]
    for j in range(1, K):
        total = total + dv[j] * nat[1, pl.ds(8 * j, 8), :]
    nat[1] = total.reshape(128, 128)

    for r in (r1w, r1f):
        r[...] = jnp.zeros_like(r)

    pl.semaphore_wait(barrier, len(peers))
    natural_start(nat.at[0], tw, pw, psw, 0)
    natural_start(nat.at[1], tf, pf, psf, 1)

    zero = jnp.zeros((2, 128, 128), F32)
    for ref in (zs, qs, ss, ds, xs, us, ws):
        ref[...] = zero
    rest = jnp.zeros((4, 128), F32)
    for t in range(2):
        for c in range(K):
            rs[t, pl.ds(8 * c, 8), :] = jnp.concatenate([nat[1, pl.ds(8 * c + t, 4, stride=2), :], rest], axis=0)

    def weight(t, j):
        return jnp.where(mask[t] > 0.0, wt[t, pl.ds(pl.multiple_of(8 * j, 8), 8), :], 0.0)

    def invert(t, fine):
        w = [weight(t, j) for j in range(K)]
        for k in range(K):
            total = (dv[0, k] * w[0]) * dv[0, : k + 1]
            for j in range(1, K):
                total = total + (dv[j, k] * w[j]) * dv[j, : k + 1]
            a[k, : k + 1] = total
            a[k, k] = a[k, k] + 4.0 * pv[t, pl.ds(8 * k, 8), :]
            if fine:
                mb[t, k, : k + 1] = a[k, : k + 1]
                if k:
                    mb[t, :k, k] = a[k, :k]

        def line(i):
            if i == K - 1:
                return a[i, : i + 1]
            return jnp.concatenate([a[i, : i + 1], a[i + 1 :, i]], axis=0)

        def put(i, value):
            a[i, : i + 1] = value[: i + 1]
            if i < K - 1:
                a[i + 1 :, i] = value[i + 1 :]

        def replaced(value, i, entry):
            parts = [value[:i], entry[None], value[i + 1 :]]
            return jnp.concatenate([part for part in parts if part.shape[0]], axis=0)

        for p in range(0, K, 2):
            q = p + 1
            col1 = line(p)
            inv1 = 1.0 / col1[p]
            sc1 = col1 * inv1
            col2 = replaced(line(q) - sc1[q] * col1, p, sc1[q])
            inv2 = 1.0 / col2[q]
            sc2 = col2 * inv2
            for i in range(K):
                if i not in (p, q):
                    a[i, : i + 1] = a[i, : i + 1] - sc1[i] * col1[: i + 1] - sc2[i] * col2[: i + 1]
            line_p = replaced(sc1 - sc2[p] * col2, p, -inv1 - sc2[p] * col2[p])
            put(p, replaced(line_p, q, sc2[p]))
            put(q, replaced(sc2, q, -inv2))
        factor = -damping * mask[t]
        for i in range(K):
            value = a[i, : i + 1] * factor
            mi[t, i, : i + 1] = value
            if i:
                mi[t, :i, i] = value[:i]

    def invert_tiles(first, stop, fine):
        def step(t, carry):
            invert(t, fine)
            return carry

        lax.fori_loop(first, stop, step, 0)

    finish(copies0(tw, pw, psw, 0))
    load0(tw, pw, wt)
    start1(wt, s1w, r1w, 0)
    invert_tiles(0, 2, True)
    finish(copies1(s1w, r1w, 0))
    load1(r1w, wt)
    start2(wt, s2w, r2w, 2)
    invert_tiles(2, 5, False)
    finish(copies2(s2w, r2w, 2))
    load2(r2w, wt)
    restrict3(wt, wt)
    invert_tiles(5, 7, False)

    def product(matrix, t, src):
        total = matrix[t, 0] * src[t, pl.ds(0, 8), :]
        for l in range(1, K):
            total = total + matrix[t, l] * src[t, pl.ds(8 * l, 8), :]
        return total.reshape(128, 128)

    STEP = 4

    def beside(level, src, g):
        def get(t):
            return src[t, pl.ds(8 * STEP * g, 8 * STEP), :].reshape(STEP, 8, 128)

        def pick(condition, x, y):
            return jnp.where(condition[None], x, y)

        if level == 0:
            e, o, h = get(0), get(1), get(2)
            y = lroll(h, 64)
            e1, o1, h1, y1 = lroll(e, 1), lroll(o, 1), lroll(h, 1), lroll(y, 1)
            em, om, hm, ym = lroll(e, -1), lroll(o, -1), lroll(h, -1), lroll(y, -1)
            start, end = lane == 0, lane == 127
            ne = o + sroll(o, 1) + pick(start, h1, e1) + pick(end, hm, em)
            no = e + sroll(e, -1) + pick(start, y1, o1) + pick(end, ym, om)
            nh = y + pick(even_half, sroll(y, 1), sroll(y, -1))
            nh = nh + pick(start, e1, pick(lane == 64, lroll(o1, 64), h1))
            nh = nh + pick(end, em, pick(lane == 63, lroll(om, 64), hm))
            return ne, no, nh
        if level == 1:
            e, o = get(3), get(4)
            ne = o + sroll(o, 1) + lroll(e, 1) + lroll(e, -1)
            no = e + sroll(e, -1) + lroll(o, 1) + lroll(o, -1)
            return ne, no
        if level == 2:
            x = get(5)
            y = lroll(x, 64)
            n = y + mask[7][None] * pick(lane < 64, sroll(y, 1), sroll(y, -1))
            return (n + lroll(x, 1) + lroll(x, -1),)
        x = get(6)
        return (mask[8][None] * sroll(x, 1) + mask[9][None] * sroll(x, -1) + lroll(x, 1) + lroll(x, -1),)

    def stencil(level, src, combine):
        for g in range(K // STEP):
            rows = pl.ds(8 * STEP * g, 8 * STEP)
            for t, n in zip(level_tiles[level], beside(level, src, g)):
                rho[t, rows, :] = combine(t, rows, pv[t, rows, :] * n.reshape(8 * STEP, 128))

    def descend(level):
        for t in level_tiles[level]:
            d1[t] = product(mi, t, fb)
        stencil(level, d1, lambda t, rows, n: keep * fb[t, rows, :] + n)
        for t in level_tiles[level]:
            value = product(mi, t, rho)
            d2[t] = value
            v[t] = d1[t] + value
        stencil(level, d2, lambda t, rows, n: keep * rho[t, rows, :] + n)

    def smooth(level, count):
        def step(i, carry):
            stencil(level, v, lambda t, rows, n: fb[t, rows, :] + n)
            for t in level_tiles[level]:
                v[t] = keep * v[t] + product(mi, t, rho)
            return carry

        lax.fori_loop(0, count, step, 0)

    up_rows = jnp.where(sub < 6, sub // 2, 7)
    up3 = lane % 64 // 2
    up2 = lane // 2 + 64 * (sub % 2)
    up1 = lane // 2 + 32
    beside_lane = jnp.where(offset < 0, (offset + 4) // 2 + 30, offset // 2 + 96)
    up1_side = jnp.where((offset >= -4) & (offset < 4), beside_lane, 0)
    sub_even = sub % 2 == 0

    def cycle(wait_first, k):
        descend(0)
        start1(rho, s1f, r1f, 1)
        wait_first()
        finish(copies1(s1f, r1f, 1))
        load1(r1f, fb)
        descend(1)
        parity = lax.rem(k, 2)
        start2(rho, s2f, r2f.at[parity], parity)
        finish(copies2(s2f, r2f.at[parity], parity))
        load2(r2f.at[parity], fb)
        descend(2)
        restrict3(rho, fb)
        v[6] = product(mi, 6, fb)
        smooth(3, 3)
        for c in range(K):
            rows = pl.ds(8 * c, 8)
            v[5, rows, :] = v[5, rows, :] + take(v[6, rows, :], up3, 1)
        smooth(2, 2)
        for c in range(K):
            rows = pl.ds(8 * c, 8)
            e = take(take(v[5, rows, :], up_rows, 0), up2, 1)
            for t in (3, 4):
                v[t, rows, :] = v[t, rows, :] + mask[t] * e
        smooth(1, 2)
        for c in range(K):
            rows = pl.ds(8 * c, 8)
            e = jnp.where(sub_even, take(v[3, rows, :], up_rows, 0), take(v[4, rows, :], up_rows, 0))
            main = take(e, up1, 1)
            v[0, rows, :] = v[0, rows, :] + main
            v[1, rows, :] = v[1, rows, :] + main
            v[2, rows, :] = v[2, rows, :] + take(e, up1_side, 1)
        smooth(0, 2)

    def copies_a(k):
        return [remote(lsend, lgx.at[k, GX - d], ags.at[k, d - 1], agr.at[k, d - 1], d, 0) for d in range(1, GX)]

    def copies_b(k):
        return [remote(lsum, lgy.at[k, GY - d], bgs.at[k, d - 1], bgr.at[k, d - 1], 0, d) for d in range(1, GY)]

    def dot(x, y):
        total = jnp.zeros((8, 128), F32)
        for t in range(2):
            for c in range(K):
                rows = pl.ds(8 * c, 8)
                total = total + x[t, rows, :] * y[t, rows, :]
        total = jnp.sum(jnp.where(sub < 4, total, 0.0), axis=0, keepdims=True)
        return jnp.sum(total, axis=1, keepdims=True)

    one_lane = lax.broadcasted_iota(jnp.int32, (1, 128), 1)

    def sum_start(k):
        gamma, delta, cross = dot(rs, us), dot(ws, us), dot(ss, us)
        lsend[...] = jnp.where(one_lane == 0, gamma, jnp.where(one_lane == 1, delta, cross))
        for copy in copies_a(k):
            copy.start()
        lgx[k, 0] = lsend[...]

    def sum_turn(k):
        finish(copies_a(k))
        total = lgx[k, 0]
        for i in range(1, GX):
            total = total + lgx[k, i]
        lsum[...] = total
        for copy in copies_b(k):
            copy.start()
        lgy[k, 0] = total

    def sum_finish(k, use_beta):
        finish(copies_b(k))
        total = lgy[k, 0]
        for i in range(1, GY):
            total = total + lgy[k, i]

        def lane_of(i):
            value = jnp.sum(jnp.where(one_lane == i, total, 0.0), axis=1, keepdims=True)
            return jnp.broadcast_to(value, (8, 128))

        gamma, delta, cross = lane_of(0), lane_of(1), lane_of(2)
        beta_now = use_beta * gamma / scal[2]
        product_now = delta + 2.0 * beta_now * cross + beta_now * beta_now * scal[3]
        scal[0] = gamma / product_now
        scal[1] = beta_now
        scal[2] = gamma
        scal[3] = product_now

    scal[0] = jnp.full((8, 128), -1.0, F32)
    scal[1] = jnp.zeros((8, 128), F32)
    scal[2] = jnp.ones((8, 128), F32)
    scal[3] = jnp.zeros((8, 128), F32)

    def trip(k, carry):
        finish(copies0(tf, pf, psf, 1))
        load0(tf, pf, fb)
        before = lax.rem(k + 1, 2)

        def turn():
            @pl.when(k > 0)
            def _():
                sum_turn(before)

        cycle(turn, k)
        stencil(0, v, lambda t, rows, n: n)
        for t in range(2):
            d1[t] = product(mb, t, v) - rho[t]

        @pl.when(k > 0)
        def _():
            sum_finish(before, jnp.where(k > 1, 1.0, 0.0))

        def update(new, old, ref, sum_ref, t, rows):
            turned = new + scal[1] * old
            ref[t, rows, :] = turned
            return turned

        for t in range(2):
            for c in range(K):
                rows = pl.ds(8 * c, 8)
                z = d1[t, rows, :] + scal[1] * zs[t, rows, :]
                zs[t, rows, :] = z
                old = ws[t, rows, :]
                ss[t, rows, :] = old + scal[1] * ss[t, rows, :]
                ws[t, rows, :] = old - scal[0] * z

        @pl.when(k < ITERS - 1)
        def _():
            for i in range(4):
                tf[pl.ds(32 * i, 16), :] = ws[0, pl.ds(i, 16, stride=8), :]
                tf[pl.ds(32 * i + 16, 16), :] = ws[1, pl.ds(i, 16, stride=8), :]
            pack(lambda c: jnp.where(sub < 4, ws[0, pl.ds(8 * c, 8), :], sroll(ws[1, pl.ds(8 * c, 8), :], 4)), psf)
            for copy in copies0(tf, pf, psf, 1):
                copy.start()

        for t in range(2):
            for c in range(K):
                rows = pl.ds(8 * c, 8)
                q = v[t, rows, :] + scal[1] * qs[t, rows, :]
                qs[t, rows, :] = q
                old = us[t, rows, :]
                d = old + scal[1] * ds[t, rows, :]
                ds[t, rows, :] = d
                xs[t, rows, :] = xs[t, rows, :] + scal[0] * d
                rs[t, rows, :] = rs[t, rows, :] - scal[0] * ss[t, rows, :]
                us[t, rows, :] = old - scal[0] * q
        sum_start(lax.rem(k, 2))
        return carry

    lax.fori_loop(0, ITERS, trip, 0)
    last_k = (ITERS - 1) % 2
    sum_turn(last_k)
    sum_finish(last_k, 1.0)
    for t in range(2):
        for c in range(K):
            rows = pl.ds(8 * c, 8)
            d = us[t, rows, :] + scal[1] * ds[t, rows, :]
            xs[t, rows, :] = xs[t, rows, :] + scal[0] * d
    for i in range(4):
        tf[pl.ds(32 * i, 16), :] = xs[0, pl.ds(i, 16, stride=8), :]
        tf[pl.ds(32 * i + 16, 16), :] = xs[1, pl.ds(i, 16, stride=8), :]
    for c in range(K):
        out[c] = tf[pl.ds(c, 8, stride=16), :]


def local(beta, design, prior, kept, removed, removed_labels):
    def vmem(*shape):
        return pltpu.VMEM(shape, F32)

    def dma(*shape):
        return pltpu.SemaphoreType.DMA(shape)

    whole = pl.BlockSpec(memory_space=pltpu.VMEM)
    scalars = pl.BlockSpec(memory_space=pltpu.SMEM)
    field = (NTILES, 128, 128)
    pair = (2, 128, 128)
    return pl.pallas_call(
        body,
        out_shape=jax.ShapeDtypeStruct(beta.shape, F32),
        in_specs=[whole, scalars, scalars, whole, whole, whole],
        out_specs=whole,
        scratch_shapes=[
            vmem(K, K, 8, 128), vmem(*field), vmem(10, 8, 128), vmem(*pair), vmem(*field),
            vmem(K, K, 8, 128), vmem(NTILES, K, K, 8, 128), vmem(2, K, K, 8, 128),
            *[vmem(*field) for _ in range(5)],
            *[vmem(*pair) for _ in range(8)], vmem(4, 8, 128),
            vmem(256, 128), vmem(256, 128), vmem(6, 8, 128), vmem(6, 8, 128), vmem(8, 128), vmem(8, 128),
            vmem(64, 128), vmem(64, 128), vmem(48, 128), vmem(48, 128), vmem(16, 128), vmem(16, 128),
            vmem(3, 128, 128), vmem(3, 128, 128), vmem(128, 128), vmem(2, 128, 128),
            vmem(1, 128), vmem(2, GX, 1, 128), vmem(2, GY, 1, 128), vmem(1, 128),
            dma(2, 8), dma(2, 8), dma(2, 8), dma(2, 8), dma(3, 7), dma(3, 7),
            dma(2, GX - 1), dma(2, GX - 1), dma(2, GY - 1), dma(2, GY - 1),
        ],
        compiler_params=pltpu.CompilerParams(collective_id=0, has_side_effects=True, vmem_limit_bytes=48 << 20),
    )(beta, design, prior, kept, removed, removed_labels)


def solution(mesh):
    placed = (
        P(None, "gx", "gy"),
        P(),
        P(),
        P(None, "gx", "gy"),
        P(None, "gx", "gy"),
        P(None, "gx", "gy"),
    )
    return jax.shard_map(
        local, mesh=mesh, in_specs=placed, out_specs=P(None, "gx", "gy"), check_vma=False
    )
```

time: 1850 us -> 114 us (0.06); the launches traced: 1820 us -> 114 us
  starting transfers between devices: 894 us -> 0 us
  blocking collectives: 513 us -> 0 us
  local copies, waits for them, and re-layouts: 149 us -> 5.34 us
  waiting for transfers between devices: 111 us -> 0 us
  Pallas kernels: 0 us -> 109 us
  other arithmetic: 104 us -> 0 us
  matrix products: 33.5 us -> 0 us
    ppermute x256 -> x0, starting transfers between devices: 894 us -> none  [the longest x128 679 us: extended(): lax.ppermute(lax.slice_in_dim(block, block.shape[dim] - width, None, axis...]
    psum x7 -> x0, blocking collectives: 513 us -> none  [the longest x4 309 us: residual_product(): return lax.psum(jnp.sum(residual * precond), ('gx', 'gy'))]
    ppermute x256 -> x0, waiting for transfers between devices: 111 us -> none  [the longest x128 106 us: extended(): lax.ppermute(lax.slice_in_dim(block, block.shape[dim] - width, None, axis...]
    pallas_call x0 -> x1, Pallas kernels: none -> 109 us  [local(): pl.pallas_call(body, out_shape=jax.ShapeDtypeStruct(beta.shape, F32), in_...]
    scatter x129 -> x0, local copies, waits for them, and re-layouts: 101 us -> none  [the longest x64 75.5 us: gauss_jordan(): scaled = blocks[pivot_at].at[pivot_at].set(1.0) / pivots[None]]
    scatter x64 -> x0, other arithmetic: 42.9 us -> none  [gauss_jordan(): blocks = blocks.at[pivot_at].set(scaled)]
    squeeze x64 -> x0, local copies, waits for them, and re-layouts: 34.6 us -> none  [gauss_jordan(): scaled = blocks[pivot_at].at[pivot_at].set(1.0) / pivots[None]]
    div x48 -> x0, other arithmetic: 33.7 us -> none  [gauss_jordan(): scaled = blocks[pivot_at].at[pivot_at].set(1.0) / pivots[None]]
  transfers between devices with their start and end apart: 256 -> 0, of which waited for: 134 -> 0; matrix products, arithmetic and copies ran while one was open for 9% -> 0% of each run, Pallas kernels for 0% -> 0%
where the time goes in v1:
time: 114 us
  Pallas kernels  109 us (96%)
  local copies, waits for them, and re-layouts  5.34 us (5%)
    pallas_call x1, Pallas kernels, local(): pl.pallas_call(body, out_shape=jax.ShapeDtypeStruct(beta.shape, F32), in_...  109 us
    unnamed x13, local copies, waits for them, and re-layouts  5.34 us

profile of v1, /device:TPU:1, one launch (start us, length us, event | category | flops | bytes accessed | tf_op | source)
XLA Modules:
  0.0 114.0 jit_solution(16188317500732883187)
XLA Ops:
  0.0 0.0 copy-start
  0.0 0.8 copy-done
  0.8 0.0 copy-start.1
  0.8 0.8 copy-done.1
  1.7 0.0 copy-start.2
  1.7 0.8 copy-done.2
  2.5 0.0 copy-start.3
  2.5 0.8 copy-done.3
  3.4 0.0 copy-start.4
  3.4 0.7 copy-done.4
  4.1 0.0 copy-start.5
  4.1 0.7 copy-done.5
  4.7 108.6 %shard_map.64 = f32[16,8,128]{2,1,0:T(8,128)S(1)} custom-call(f32[16,8,128]{2,1,0:T(8,128)S(1)} %copy-done, f32[16,16]{1,0:T(8,128)S(1)} %copy-done.4, f32[16]{0:T(128)S(1)} %copy-done.5, s32[16,8,128]{2,1,0:T(8,128)S(1)} %copy-done.1, s32[16,8,128]{2,1,0:T(8,128)S(1)} %copy-done.2, s32[16,8,128]{2,1,0:T(8,128)S(1)} %copy-done.3), custom_call_target="tpu_custom_call" | custom-call | tf_op jit(solution)/shard_map/pallas_call | solution.py:564
  113.3 0.6 copy.8
Async XLA Ops:
  0.0 0.8 copy-start
  0.8 0.8 copy-start.1
  1.7 0.8 copy-start.2
  2.5 0.8 copy-start.3
  3.4 0.7 copy-start.4
  4.1 0.7 copy-start.5

commit v2 on v1

--- a/solution.py
+++ b/solution.py
@@ -37,19 +37,36 @@
 
 
 def body(
-    beta, design, prior, kept, removed, labels, out,
-    dv, pv, mask, nat, wt, a, mi, mb,
+    beta_in, design_in, prior_in, kept_in, removed_in, labels_in, out,
+    beta, design, prior, kept, removed, labels, insem, dv, pv, mask, nat, wt, a, mi, mb,
     fb, d1, d2, rho, v,
     zs, qs, ss, ds, xs, rs, us, ws, scal,
     tw, tf, pw, pf, psw, psf, g1b, g2b, s1w, s1f, s2w, s2f, r1w, r1f, r2w, r2f,
-    lsend, lgx, lgy, lsum,
-    e0s, e0r, e1s, e1r, e2s, e2r, ags, agr, bgs, bgr,
+    lsend, lgx, lgy, lsum, lall,
+    e0s, e0r, e1s, e1r, e2s, e2r, ags, agr, bgs, bgr, alls, allr,
 ):
     mx, my = lax.axis_index("gx"), lax.axis_index("gy")
     sub, lane = iota(0), iota(1)
 
     def device(dx, dy):
         return (lax.rem(mx + dx + GX, GX), lax.rem(my + dy + GY, GY))
+
+    inputs = [
+        pltpu.make_async_copy(src, dst, insem.at[i])
+        for i, (src, dst) in enumerate(
+            (
+                (design_in, design), (prior_in, prior), (beta_in, beta),
+                (kept_in, kept), (removed_in, removed), (labels_in, labels),
+            )
+        )
+    ]
+    for copy in inputs:
+        copy.start()
+
+    for r in (r1w, r1f, pw, pf):
+        r[...] = jnp.zeros_like(r)
+    for t in (tw, tf):
+        t[pl.ds(128, 128), :] = jnp.zeros((128, 128), F32)
 
     barrier = pltpu.get_barrier_semaphore()
     peers = [(d, 0) for d in range(1, GX)] + [(0, d) for d in range(1, GY)]
@@ -57,20 +74,40 @@
     for dx, dy in peers:
         pl.semaphore_signal(barrier, inc=1, device_id=device(dx, dy), device_id_type=MESH)
 
+    has = {-1: mx > 0, 1: mx < GX - 1}
+    has_y = {-1: my > 0, 1: my < GY - 1}
+
+    def exists(dx, dy):
+        found = [table[d] for table, d in ((has, dx), (has_y, dy)) if d]
+        return found[0] if len(found) == 1 else found[0] & found[1]
+
     def remote(src, dst, ssem, rsem, dx, dy):
         return pltpu.make_async_remote_copy(
             src_ref=src, dst_ref=dst, send_sem=ssem, recv_sem=rsem, device_id=device(dx, dy), device_id_type=MESH
         )
 
     def copies0(t, p, ps, k):
-        out = [
-            remote(t.at[pl.ds(0, 64)], t.at[pl.ds(128, 64)], e0s.at[k, 0], e0r.at[k, 0], -1, 0),
-            remote(t.at[pl.ds(64, 64)], t.at[pl.ds(192, 64)], e0s.at[k, 1], e0r.at[k, 1], 1, 0),
-        ]
+        out = []
         for j, (dx, dy) in enumerate(sideways):
             slot = sideways.index((-dx, -dy))
-            out.append(remote(ps, p.at[slot], e0s.at[k, 2 + j], e0r.at[k, 2 + j], dx, dy))
+            out.append((remote(ps, p.at[slot], e0s.at[k, 2 + j], e0r.at[k, 2 + j], dx, dy), dx, dy))
+        out.append((remote(t.at[pl.ds(0, 64)], t.at[pl.ds(128, 64)], e0s.at[k, 0], e0r.at[k, 0], -1, 0), -1, 0))
+        out.append((remote(t.at[pl.ds(64, 64)], t.at[pl.ds(192, 64)], e0s.at[k, 1], e0r.at[k, 1], 1, 0), 1, 0))
         return out
+
+    def start(copies):
+        for copy, dx, dy in copies:
+            pl.when(exists(dx, dy))(copy.start)
+
+    def finish(copies):
+        for copy, dx, dy in copies:
+            pl.when(exists(-dx, -dy))(copy.wait_recv)
+        for copy, dx, dy in copies:
+            pl.when(exists(dx, dy))(copy.wait_send)
+
+    def finish_all(copy):
+        copy.wait_recv()
+        copy.wait_send()
 
     group = (lane + 4) // 8 % 16
     right_side = lane % 8 < 4
@@ -99,8 +136,7 @@
         for r in range(8):
             t[pl.ds(16 * r, 16), :] = src[pl.ds(r, 16, stride=8), :]
         pack(lambda c: jnp.concatenate([src[pl.ds(8 * c + i, 4, stride=2), :] for i in range(2)], axis=0), ps)
-        for copy in copies0(t, p, ps, k):
-            copy.start()
+        start(copies0(t, p, ps, k))
 
     lane_even = lane % 2 == 0
     split = jnp.where(lane < 64, 2 * lane, 2 * (lane - 64) + 1)
@@ -115,10 +151,9 @@
         rows = {1: (0, 40, 88), -1: (8, 40, 32), 0: (8, 32, 0)}
         out = []
         for j, (dx, dy) in enumerate(around):
-            start, size, target = rows[dx]
-            out.append(
-                remote(s.at[pl.ds(start, size)], r.at[1 - dy, pl.ds(target, size)], e1s.at[k, j], e1r.at[k, j], dx, dy)
-            )
+            first, size, target = rows[dx]
+            src, dst = s.at[pl.ds(first, size)], r.at[1 - dy, pl.ds(target, size)]
+            out.append((remote(src, dst, e1s.at[k, j], e1r.at[k, j], dx, dy), dx, dy))
         return out
 
     def start1(src, s, r, k):
@@ -126,8 +161,7 @@
         s[pl.ds(0, 8), :] = g1b[pl.ds(7, 8, stride=8), :]
         for i in range(5):
             s[pl.ds(8 + 8 * i, 8), :] = g1b[pl.ds(i, 8, stride=8), :]
-        for copy in copies1(s, r, k):
-            copy.start()
+        start(copies1(s, r, k))
         r[1, pl.ds(0, 32), :] = s[pl.ds(8, 32), :]
 
     middle = (lane >= 32) & (lane < 96)
@@ -143,8 +177,12 @@
 
     def copies2(s, r, k):
         return [
-            remote(s, r.at[pl.ds(16 * (GX - d), 16)], e2s.at[k, d - 1], e2r.at[k, d - 1], d, 0) for d in range(1, GX)
+            remote(s, r.at[pl.ds(16 * (GX - d), 16)], e2s.at[k], e2r.at[k], d, 0) for d in range(1, GX)
         ]
+
+    def finish2(r, k):
+        rest = r.at[pl.ds(16, 16 * (GX - 1))]
+        finish_all(remote(rest, rest, e2s.at[k], e2r.at[k], 1, 0))
 
     def start2(src, s, r, k):
         restrict_pairs(src, 3, g2b)
@@ -160,12 +198,6 @@
             dst[5, pl.ds(8 * c, 8), :] = jnp.where(lane < 64, even, lroll(odd, 64))
             dst[5, pl.ds(8 * c + 64, 8), :] = jnp.where(lane < 64, lroll(even, 64), odd)
 
-    def finish(copies):
-        for copy in copies:
-            copy.wait_recv()
-        for copy in copies:
-            copy.wait_send()
-
     twice = 2 * lane % 64
 
     def restrict3(src, dst):
@@ -173,16 +205,6 @@
             x = src[5, pl.ds(8 * c, 8), :]
             x = x + lroll(x, 64)
             dst[6, pl.ds(8 * c, 8), :] = take(x + lroll(x, -1), twice, 1)
-
-    def fill(j, carry):
-        for k in range(K):
-            dv[j, k] = jnp.full((8, 128), design[j, k], F32)
-        return carry
-
-    lax.fori_loop(0, K, fill, 0)
-    for t in range(NTILES):
-        for k in range(K):
-            pv[t, pl.ds(8 * k, 8), :] = jnp.full((8, 128), prior[k] * 2.0 ** tile_level[t], F32)
 
     def one(condition):
         return jnp.where(condition, 1.0, 0.0).astype(F32)
@@ -217,6 +239,19 @@
     mask[8] = one(~first)
     mask[9] = one(~last)
 
+    for copy in inputs:
+        copy.wait()
+
+    def fill(j, carry):
+        for k in range(K):
+            dv[j, k] = jnp.full((8, 128), design[j, k], F32)
+        return carry
+
+    lax.fori_loop(0, K, fill, 0)
+    for t in range(NTILES):
+        for k in range(K):
+            pv[t, pl.ds(8 * k, 8), :] = jnp.full((8, 128), prior[k] * 2.0 ** tile_level[t], F32)
+
     logits = dv[:, 0] * beta[0]
     for k in range(1, K):
         logits = logits + dv[:, k] * beta[k]
@@ -228,8 +263,6 @@
         total = total + dv[j] * nat[1, pl.ds(8 * j, 8), :]
     nat[1] = total.reshape(128, 128)
 
-    for r in (r1w, r1f):
-        r[...] = jnp.zeros_like(r)
 
     pl.semaphore_wait(barrier, len(peers))
     natural_start(nat.at[0], tw, pw, psw, 0)
@@ -246,7 +279,7 @@
     def weight(t, j):
         return jnp.where(mask[t] > 0.0, wt[t, pl.ds(pl.multiple_of(8 * j, 8), 8), :], 0.0)
 
-    def invert(t, fine):
+    def invert(t):
         w = [weight(t, j) for j in range(K)]
         for k in range(K):
             total = (dv[0, k] * w[0]) * dv[0, : k + 1]
@@ -254,7 +287,10 @@
                 total = total + (dv[j, k] * w[j]) * dv[j, : k + 1]
             a[k, : k + 1] = total
             a[k, k] = a[k, k] + 4.0 * pv[t, pl.ds(8 * k, 8), :]
-            if fine:
+
+        @pl.when(t < 2)
+        def _():
+            for k in range(K):
                 mb[t, k, : k + 1] = a[k, : k + 1]
                 if k:
                     mb[t, :k, k] = a[k, :k]
@@ -294,9 +330,9 @@
             if i:
                 mi[t, :i, i] = value[:i]
 
-    def invert_tiles(first, stop, fine):
+    def invert_tiles(first, stop):
         def step(t, carry):
-            invert(t, fine)
+            invert(t)
             return carry
 
         lax.fori_loop(first, stop, step, 0)
@@ -304,15 +340,10 @@
     finish(copies0(tw, pw, psw, 0))
     load0(tw, pw, wt)
     start1(wt, s1w, r1w, 0)
-    invert_tiles(0, 2, True)
+    invert_tiles(0, 3)
     finish(copies1(s1w, r1w, 0))
     load1(r1w, wt)
     start2(wt, s2w, r2w, 2)
-    invert_tiles(2, 5, False)
-    finish(copies2(s2w, r2w, 2))
-    load2(r2w, wt)
-    restrict3(wt, wt)
-    invert_tiles(5, 7, False)
 
     def product(matrix, t, src):
         total = matrix[t, 0] * src[t, pl.ds(0, 8), :]
@@ -387,7 +418,7 @@
     up1_side = jnp.where((offset >= -4) & (offset < 4), beside_lane, 0)
     sub_even = sub % 2 == 0
 
-    def cycle(wait_first, k):
+    def cycle(wait_first, wait_second, k):
         descend(0)
         start1(rho, s1f, r1f, 1)
         wait_first()
@@ -396,7 +427,8 @@
         descend(1)
         parity = lax.rem(k, 2)
         start2(rho, s2f, r2f.at[parity], parity)
-        finish(copies2(s2f, r2f.at[parity], parity))
+        wait_second()
+        finish2(r2f.at[parity], parity)
         load2(r2f.at[parity], fb)
         descend(2)
         restrict3(rho, fb)
@@ -422,10 +454,14 @@
         smooth(0, 2)
 
     def copies_a(k):
-        return [remote(lsend, lgx.at[k, GX - d], ags.at[k, d - 1], agr.at[k, d - 1], d, 0) for d in range(1, GX)]
+        return [remote(lsend, lgx.at[k, GX - d], ags.at[k], agr.at[k], d, 0) for d in range(1, GX)]
 
     def copies_b(k):
-        return [remote(lsum, lgy.at[k, GY - d], bgs.at[k, d - 1], bgr.at[k, d - 1], 0, d) for d in range(1, GY)]
+        return [remote(lsum, lgy.at[k, GY - d], bgs.at[k], bgr.at[k], 0, d) for d in range(1, GY)]
+
+    def finish_sum(landing, count, ssem, rsem):
+        rest = landing.at[pl.ds(1, count - 1)]
+        finish_all(remote(rest, rest, ssem, rsem, 0, 1))
 
     def dot(x, y):
         total = jnp.zeros((8, 128), F32)
@@ -438,15 +474,18 @@
 
     one_lane = lax.broadcasted_iota(jnp.int32, (1, 128), 1)
 
-    def sum_start(k):
+    def sum_parts():
         gamma, delta, cross = dot(rs, us), dot(ws, us), dot(ss, us)
         lsend[...] = jnp.where(one_lane == 0, gamma, jnp.where(one_lane == 1, delta, cross))
+
+    def sum_start(k):
+        sum_parts()
         for copy in copies_a(k):
             copy.start()
         lgx[k, 0] = lsend[...]
 
     def sum_turn(k):
-        finish(copies_a(k))
+        finish_sum(lgx.at[k], GX, ags.at[k], agr.at[k])
         total = lgx[k, 0]
         for i in range(1, GX):
             total = total + lgx[k, i]
@@ -456,10 +495,20 @@
         lgy[k, 0] = total
 
     def sum_finish(k, use_beta):
-        finish(copies_b(k))
-        total = lgy[k, 0]
-        for i in range(1, GY):
-            total = total + lgy[k, i]
+        finish_sum(lgy.at[k], GY, bgs.at[k], bgr.at[k])
+        scalars(jnp.sum(lgy[k], axis=0), use_beta)
+
+    def sum_at_once():
+        sum_parts()
+        for d in range(1, GX * GY):
+            dx, dy = d // GY, d % GY
+            slot = (GX - dx) % GX * GY + (GY - dy) % GY
+            remote(lsend, lall.at[slot], alls, allr, dx, dy).start()
+        lall[0] = lsend[...]
+        finish_sum(lall, GX * GY, alls, allr)
+        scalars(jnp.sum(lall[...], axis=0), 1.0)
+
+    def scalars(total, use_beta):
 
         def lane_of(i):
             value = jnp.sum(jnp.where(one_lane == i, total, 0.0), axis=1, keepdims=True)
@@ -488,7 +537,19 @@
             def _():
                 sum_turn(before)
 
-        cycle(turn, k)
+            @pl.when(k == 0)
+            def _():
+                invert_tiles(3, 5)
+                finish2(r2w, 2)
+                load2(r2w, wt)
+                restrict3(wt, wt)
+
+        def coarse():
+            @pl.when(k == 0)
+            def _():
+                invert_tiles(5, 7)
+
+        cycle(turn, coarse, k)
         stencil(0, v, lambda t, rows, n: n)
         for t in range(2):
             d1[t] = product(mb, t, v) - rho[t]
@@ -517,8 +578,7 @@
                 tf[pl.ds(32 * i, 16), :] = ws[0, pl.ds(i, 16, stride=8), :]
                 tf[pl.ds(32 * i + 16, 16), :] = ws[1, pl.ds(i, 16, stride=8), :]
             pack(lambda c: jnp.where(sub < 4, ws[0, pl.ds(8 * c, 8), :], sroll(ws[1, pl.ds(8 * c, 8), :], 4)), psf)
-            for copy in copies0(tf, pf, psf, 1):
-                copy.start()
+            start(copies0(tf, pf, psf, 1))
 
         for t in range(2):
             for c in range(K):
@@ -531,13 +591,15 @@
                 xs[t, rows, :] = xs[t, rows, :] + scal[0] * d
                 rs[t, rows, :] = rs[t, rows, :] - scal[0] * ss[t, rows, :]
                 us[t, rows, :] = old - scal[0] * q
-        sum_start(lax.rem(k, 2))
+
+        @pl.when(k < ITERS - 1)
+        def _():
+            sum_start(lax.rem(k, 2))
+
         return carry
 
     lax.fori_loop(0, ITERS, trip, 0)
-    last_k = (ITERS - 1) % 2
-    sum_turn(last_k)
-    sum_finish(last_k, 1.0)
+    sum_at_once()
     for t in range(2):
         for c in range(K):
             rows = pl.ds(8 * c, 8)
@@ -558,15 +620,17 @@
         return pltpu.SemaphoreType.DMA(shape)
 
     whole = pl.BlockSpec(memory_space=pltpu.VMEM)
-    scalars = pl.BlockSpec(memory_space=pltpu.SMEM)
+    outside = pl.BlockSpec(memory_space=pltpu.HBM)
+    counts = pltpu.VMEM((K, 8, 128), jnp.int32)
     field = (NTILES, 128, 128)
     pair = (2, 128, 128)
     return pl.pallas_call(
         body,
         out_shape=jax.ShapeDtypeStruct(beta.shape, F32),
-        in_specs=[whole, scalars, scalars, whole, whole, whole],
+        in_specs=[outside] * 6,
         out_specs=whole,
         scratch_shapes=[
+            vmem(K, 8, 128), pltpu.SMEM((K, K), F32), pltpu.SMEM((K,), F32), counts, counts, counts, dma(6),
             vmem(K, K, 8, 128), vmem(*field), vmem(10, 8, 128), vmem(*pair), vmem(*field),
             vmem(K, K, 8, 128), vmem(NTILES, K, K, 8, 128), vmem(2, K, K, 8, 128),
             *[vmem(*field) for _ in range(5)],
@@ -574,9 +638,9 @@
             vmem(256, 128), vmem(256, 128), vmem(6, 8, 128), vmem(6, 8, 128), vmem(8, 128), vmem(8, 128),
             vmem(64, 128), vmem(64, 128), vmem(48, 128), vmem(48, 128), vmem(16, 128), vmem(16, 128),
             vmem(3, 128, 128), vmem(3, 128, 128), vmem(128, 128), vmem(2, 128, 128),
-            vmem(1, 128), vmem(2, GX, 1, 128), vmem(2, GY, 1, 128), vmem(1, 128),
-            dma(2, 8), dma(2, 8), dma(2, 8), dma(2, 8), dma(3, 7), dma(3, 7),
-            dma(2, GX - 1), dma(2, GX - 1), dma(2, GY - 1), dma(2, GY - 1),
+            vmem(1, 128), vmem(2, GX, 1, 128), vmem(2, GY, 1, 128), vmem(1, 128), vmem(GX * GY, 1, 128),
+            dma(2, 8), dma(2, 8), dma(2, 8), dma(2, 8), dma(3), dma(3), dma(2), dma(2), dma(2), dma(2),
+            pltpu.SemaphoreType.DMA, pltpu.SemaphoreType.DMA,
         ],
         compiler_params=pltpu.CompilerParams(collective_id=0, has_side_effects=True, vmem_limit_bytes=48 << 20),
     )(beta, design, prior, kept, removed, removed_labels)

time: 114 us -> 95.1 us (0.83)
  Pallas kernels: 109 us -> 89.4 us
    pallas_call x1, Pallas kernels: 109 us -> 89.4 us  [local(): pl.pallas_call(body, out_shape=jax.ShapeDtypeStruct(beta.shape, F32), in_...]
where the time goes in v2:
time: 95.1 us; the launch traced here: 94.7 us
  Pallas kernels  89.4 us (94%)
  local copies, waits for them, and re-layouts  5.34 us (6%)
    pallas_call x1, Pallas kernels, local(): pl.pallas_call(body, out_shape=jax.ShapeDtypeStruct(beta.shape, F32), in_...  89.4 us
    unnamed x13, local copies, waits for them, and re-layouts  5.34 us

profile of v2, /device:TPU:1, one launch (start us, length us, event | category | flops | bytes accessed | tf_op | source)
XLA Modules:
  0.0 94.7 jit_solution(1933817570916259929)
XLA Ops:
  0.0 0.0 copy-start
  0.0 0.8 copy-done
  0.8 0.0 copy-start.1
  0.8 0.8 copy-done.1
  1.7 0.0 copy-start.2
  1.7 0.8 copy-done.2
  2.5 0.0 copy-start.3
  2.5 0.8 copy-done.3
  3.4 0.0 copy-start.4
  3.4 0.7 copy-done.4
  4.1 0.0 copy-start.5
  4.1 0.7 copy-done.5
  4.7 89.4 %shard_map.64 = f32[16,8,128]{2,1,0:T(8,128)S(1)} custom-call(f32[16,8,128]{2,1,0:T(8,128)S(1)} %copy-done, f32[16,16]{1,0:T(8,128)S(1)} %copy-done.4, f32[16]{0:T(128)S(1)} %copy-done.5, s32[16,8,128]{2,1,0:T(8,128)S(1)} %copy-done.1, s32[16,8,128]{2,1,0:T(8,128)S(1)} %copy-done.2, s32[16,8,128]{2,1,0:T(8,128)S(1)} %copy-done.3), custom_call_target="tpu_custom_call" | custom-call | tf_op jit(solution)/shard_map/pallas_call | solution.py:627
  94.1 0.6 copy.8
Async XLA Ops:
  0.0 0.8 copy-start
  0.8 0.8 copy-start.1
  1.7 0.8 copy-start.2
  2.5 0.8 copy-start.3
  3.4 0.7 copy-start.4
  4.1 0.7 copy-start.5

commit v3 on v2

--- a/solution.py
+++ b/solution.py
@@ -16,8 +16,8 @@
 
 level_tiles = {0: (0, 1, 2), 1: (3, 4), 2: (5,), 3: (6,)}
 tile_level = (0, 0, 0, 1, 1, 2, 3)
-around = ((-1, -1), (-1, 0), (-1, 1), (0, -1), (0, 1), (1, -1), (1, 0), (1, 1))
-sideways = tuple(o for o in around if o[1] != 0)
+sideways = ((-1, -1), (-1, 1), (1, -1), (1, 1), (0, -1), (0, 1))
+around = sideways + ((-1, 0), (1, 0))
 
 
 def iota(axis):
@@ -41,7 +41,7 @@
     beta, design, prior, kept, removed, labels, insem, dv, pv, mask, nat, wt, a, mi, mb,
     fb, d1, d2, rho, v,
     zs, qs, ss, ds, xs, rs, us, ws, scal,
-    tw, tf, pw, pf, psw, psf, g1b, g2b, s1w, s1f, s2w, s2f, r1w, r1f, r2w, r2f,
+    tw, tf, th, pw, pf, psw, psf, g1b, g2b, gs, s1w, s1f, ssw, ssf, s2w, s2f, r1w, r1f, rsw, rsf, r2w, r2f,
     lsend, lgx, lgy, lsum, lall,
     e0s, e0r, e1s, e1r, e2s, e2r, ags, agr, bgs, bgr, alls, allr,
 ):
@@ -50,6 +50,27 @@
 
     def device(dx, dy):
         return (lax.rem(mx + dx + GX, GX), lax.rem(my + dy + GY, GY))
+
+    barrier = pltpu.get_barrier_semaphore()
+    has = {-1: mx > 0, 1: mx < GX - 1}
+    has_y = {-1: my > 0, 1: my < GY - 1}
+
+    def exists(dx, dy):
+        found = [table[d] for table, d in ((has, dx), (has_y, dy)) if d]
+        return found[0] if len(found) == 1 else found[0] & found[1]
+
+    def signal(dx, dy):
+        pl.semaphore_signal(barrier, inc=1, device_id=device(dx, dy), device_id_type=MESH)
+
+    corners = tuple(o for o in sideways if o[0] != 0)
+    for dx, dy in corners:
+        pl.when(exists(dx, dy))(lambda dx=dx, dy=dy: signal(dx, dy))
+    greeted = [(0, d) for d in (1, 15, 4, 12, 8, 6, 10)] + [(d, 0) for d in range(1, GX)]
+    for dx, dy in greeted:
+        signal(dx, dy)
+    beside_x = jnp.where((mx > 0) & (mx < GX - 1), 2, 1)
+    beside_y = jnp.where((my > 0) & (my < GY - 1), 2, 1)
+    peers = len(greeted) + beside_x * beside_y
 
     inputs = [
         pltpu.make_async_copy(src, dst, insem.at[i])
@@ -63,23 +84,23 @@
     for copy in inputs:
         copy.start()
 
-    for r in (r1w, r1f, pw, pf):
+    def clear(dx, dy):
+        slot = sideways.index((dx, dy))
+        for p in (pw, pf):
+            p[slot] = jnp.zeros((32, 128), F32)
+
+    for dx, dy in sideways:
+        pl.when(~exists(dx, dy))(lambda dx=dx, dy=dy: clear(dx, dy))
+
+    def clear_rows(i):
+        for t in (tw, tf):
+            t[pl.ds(128 + 64 * i, 64), :] = jnp.zeros((64, 128), F32)
+        th[pl.ds(64 + 32 * i, 32), :] = jnp.zeros((32, 128), F32)
+
+    pl.when(~has[1])(lambda: clear_rows(0))
+    pl.when(~has[-1])(lambda: clear_rows(1))
+    for r in (r1w, r1f, rsw, rsf):
         r[...] = jnp.zeros_like(r)
-    for t in (tw, tf):
-        t[pl.ds(128, 128), :] = jnp.zeros((128, 128), F32)
-
-    barrier = pltpu.get_barrier_semaphore()
-    peers = [(d, 0) for d in range(1, GX)] + [(0, d) for d in range(1, GY)]
-    peers += [o for o in around if o[0] != 0 and o[1] != 0]
-    for dx, dy in peers:
-        pl.semaphore_signal(barrier, inc=1, device_id=device(dx, dy), device_id_type=MESH)
-
-    has = {-1: mx > 0, 1: mx < GX - 1}
-    has_y = {-1: my > 0, 1: my < GY - 1}
-
-    def exists(dx, dy):
-        found = [table[d] for table, d in ((has, dx), (has_y, dy)) if d]
-        return found[0] if len(found) == 1 else found[0] & found[1]
 
     def remote(src, dst, ssem, rsem, dx, dy):
         return pltpu.make_async_remote_copy(
@@ -109,34 +130,50 @@
         copy.wait_recv()
         copy.wait_send()
 
-    group = (lane + 4) // 8 % 16
-    right_side = lane % 8 < 4
+    group = (lane + 16) // 32 % 4
+    right_side = lane % 32 < 16
     even_half = (lane < 32) | (lane >= 96)
 
     def pack(rows_of, ps):
-        total = jnp.zeros((8, 128), F32)
-        for c in range(K):
-            x = rows_of(c)
-            total = jnp.where(group == c, lroll(x, 8 * c), total)
-        ps[...] = total
-
-    def load0(t, p, dst):
-        def merged(dx):
-            return jnp.where(right_side, p[sideways.index((dx, 1))], p[sideways.index((dx, -1))])
-
-        here, below, above = merged(0), merged(1), merged(-1)
-        even = jnp.where(sub < 4, here, sroll(jnp.where(sub < 2, below, above), 4))
-        odd = jnp.where(sub < 4, sroll(here, 4), jnp.where(sub < 6, below, above))
+        for q in range(4):
+            total = rows_of(4 * q)
+            for j in range(1, 4):
+                total = jnp.where(group == j, lroll(rows_of(4 * q + j), 32 * j), total)
+            ps[pl.ds(8 * q, 8), :] = total
+
+    def load_main(t, dst):
         for c in range(K):
             dst[0, pl.ds(8 * c, 8), :] = t[pl.ds(c, 8, stride=32), :]
             dst[1, pl.ds(8 * c, 8), :] = t[pl.ds(16 + c, 8, stride=32), :]
-            dst[2, pl.ds(8 * c, 8), :] = jnp.where(even_half, lroll(even, -8 * c), lroll(odd, 64 - 8 * c))
-
-    def natural_start(src, t, p, ps, k):
+
+    def load0(t, p, dst):
+        load_main(t, dst)
+        for q in range(4):
+            rows = pl.ds(8 * q, 8)
+
+            def merged(dx):
+                return jnp.where(right_side, p[sideways.index((dx, 1)), rows, :], p[sideways.index((dx, -1)), rows, :])
+
+            here, below, above = merged(0), merged(1), merged(-1)
+            even = jnp.where(sub < 4, here, sroll(jnp.where(sub < 2, below, above), 4))
+            odd = jnp.where(sub < 4, sroll(here, 4), jnp.where(sub < 6, below, above))
+            for j in range(4):
+                side = jnp.where(even_half, lroll(even, -32 * j), lroll(odd, 64 - 32 * j))
+                dst[2, pl.ds(8 * (4 * q + j), 8), :] = side
+
+    def natural_prepare(src, t, ps):
+        pack(lambda c: jnp.concatenate([src[pl.ds(8 * c + i, 4, stride=2), :] for i in range(2)], axis=0), ps)
         for r in range(8):
             t[pl.ds(16 * r, 16), :] = src[pl.ds(r, 16, stride=8), :]
-        pack(lambda c: jnp.concatenate([src[pl.ds(8 * c + i, 4, stride=2), :] for i in range(2)], axis=0), ps)
-        start(copies0(t, p, ps, k))
+
+    def copies_again():
+        out = []
+        for i, dx in enumerate((-1, 1)):
+            src, dst = tf.at[pl.ds(64 * i, 64)], tf.at[pl.ds(128 + 64 * i, 64)]
+            out.append((remote(src, dst, e0s.at[2, i], e0r.at[2, i], dx, 0), dx, 0))
+            src, dst = th.at[pl.ds(32 * i, 32)], th.at[pl.ds(64 + 32 * i, 32)]
+            out.append((remote(src, dst, e0s.at[2, 2 + i], e0r.at[2, 2 + i], dx, 0), dx, 0))
+        return out
 
     lane_even = lane % 2 == 0
     split = jnp.where(lane < 64, 2 * lane, 2 * (lane - 64) + 1)
@@ -147,33 +184,45 @@
             hi = src[first, pl.ds(8 * c + 64, 8), :] + src[first + 1, pl.ds(8 * c + 64, 8), :]
             g[pl.ds(8 * c, 8), :] = take(jnp.where(lane_even, lo + lroll(lo, -1), hi + lroll(hi, 1)), split, 1)
 
-    def copies1(s, r, k):
-        rows = {1: (0, 40, 88), -1: (8, 40, 32), 0: (8, 32, 0)}
+    def copies1(s, sides, r, rsides, k):
+        side_rows = {1: (0, 24, 40), -1: (8, 24, 16), 0: (8, 16, 0)}
         out = []
-        for j, (dx, dy) in enumerate(around):
-            first, size, target = rows[dx]
-            src, dst = s.at[pl.ds(first, size)], r.at[1 - dy, pl.ds(target, size)]
+        for j, (dx, dy) in enumerate(sideways):
+            first, size, target = side_rows[dx]
+            slot = 0 if dy == 1 else 1
+            src, dst = sides.at[slot, pl.ds(first, size)], rsides.at[slot, pl.ds(target, size)]
             out.append((remote(src, dst, e1s.at[k, j], e1r.at[k, j], dx, dy), dx, dy))
+        for j, (dx, first, target) in enumerate(((-1, 8, 32), (1, 0, 88))):
+            src, dst = s.at[pl.ds(first, 40)], r.at[pl.ds(target, 40)]
+            out.append((remote(src, dst, e1s.at[k, 6 + j], e1r.at[k, 6 + j], dx, 0), dx, 0))
         return out
 
-    def start1(src, s, r, k):
+    middle = (lane >= 32) & (lane < 96)
+    high = (lane // 32) % 2 == 1
+
+    def start1(src, s, sides, r, rsides, k):
         restrict_pairs(src, 0, g1b)
-        s[pl.ds(0, 8), :] = g1b[pl.ds(7, 8, stride=8), :]
-        for i in range(5):
-            s[pl.ds(8 + 8 * i, 8), :] = g1b[pl.ds(i, 8, stride=8), :]
-        start(copies1(s, r, k))
-        r[1, pl.ds(0, 32), :] = s[pl.ds(8, 32), :]
-
-    middle = (lane >= 32) & (lane < 96)
-    from_left = (lane // 32) % 2 == 1
-
-    def load1(r, dst):
-        for tile, base in ((3, 0), (4, 8)):
-            for c in range(8):
-                left, here, right = (r[g, pl.ds(base + c, 8, stride=16), :] for g in range(3))
-                side = jnp.where(from_left, left, right)
-                dst[tile, pl.ds(8 * c, 8), :] = jnp.where(middle, lroll(here, 32), lroll(side, 96))
-                dst[tile, pl.ds(8 * c + 64, 8), :] = jnp.where(middle, lroll(here, 96), lroll(side, 32))
+        for c in range(4):
+            first, second = g1b[pl.ds(8 * c, 8), :], lroll(g1b[pl.ds(8 * c + 32, 8), :], 32)
+            gs[0, pl.ds(8 * c, 8), :] = jnp.where(high, first, second)
+            gs[1, pl.ds(8 * c, 8), :] = jnp.where(high, second, first)
+        for i in range(8):
+            for slot in range(2):
+                sides[slot, pl.ds(4 * i, 4), :] = gs[slot, pl.ds((i + 6) % 8, 4, stride=8), :]
+        for i in range(6):
+            s[pl.ds(8 * i, 8), :] = g1b[pl.ds((i + 7) % 8, 8, stride=8), :]
+        start(copies1(s, sides, r, rsides, k))
+        r[pl.ds(0, 32), :] = s[pl.ds(8, 32), :]
+
+    def load1(r, rsides, dst):
+        for tile, base in ((3, 0), (4, 1)):
+            for c in range(4):
+                left, right = (rsides[i, pl.ds(4 * base + c, 8, stride=8), :] for i in range(2))
+                here = [r[pl.ds(8 * base + c + 4 * i, 8, stride=16), :] for i in range(2)]
+                for j in range(4):
+                    side = lroll(jnp.where(lane // 32 == j, right, left), 96 - 32 * j)
+                    center = lroll(here[j % 2], 32 if j < 2 else 96)
+                    dst[tile, pl.ds(8 * (c + 4 * j), 8), :] = jnp.where(middle, center, side)
 
     def copies2(s, r, k):
         return [
@@ -217,7 +266,7 @@
     at = 8 * mx + row
     offset = (lane + 32) % 64 - 32
     column = 128 * my + jnp.where(offset < 0, offset, 128 + offset)
-    mask[2] = one((at >= 0) & (at < 64) & (offset >= -4) & (offset < 4) & (column >= 0) & (column < 2048))
+    mask[2] = one((at >= 0) & (at < 64) & (offset >= -16) & (offset < 16) & (column >= 0) & (column < 2048))
     for t in range(2):
         row = jnp.where(sub < 5, 2 * sub, 2 * sub - 16) + t
         at = 4 * mx + row
@@ -239,7 +288,7 @@
     mask[8] = one(~first)
     mask[9] = one(~last)
 
-    for copy in inputs:
+    for copy in inputs[:2]:
         copy.wait()
 
     def fill(j, carry):
@@ -248,29 +297,31 @@
         return carry
 
     lax.fori_loop(0, K, fill, 0)
-    for t in range(NTILES):
-        for k in range(K):
-            pv[t, pl.ds(8 * k, 8), :] = jnp.full((8, 128), prior[k] * 2.0 ** tile_level[t], F32)
-
+
+    for copy in inputs[2:]:
+        copy.wait()
     logits = dv[:, 0] * beta[0]
     for k in range(1, K):
         logits = logits + dv[:, k] * beta[k]
     prob = 1.0 / (1.0 + jnp.exp(-logits))
     nat[0] = (kept[...].astype(F32) * prob * (1.0 - prob)).reshape(128, 128)
     nat[1] = (removed[...].astype(F32) * prob - labels[...].astype(F32)).reshape(128, 128)
+    natural_prepare(nat.at[0], tw, psw)
+    pl.semaphore_wait(barrier, peers)
+    start(copies0(tw, pw, psw, 0))
+
     total = dv[0] * nat[1, pl.ds(0, 8), :]
     for j in range(1, K):
         total = total + dv[j] * nat[1, pl.ds(8 * j, 8), :]
     nat[1] = total.reshape(128, 128)
-
-
-    pl.semaphore_wait(barrier, len(peers))
-    natural_start(nat.at[0], tw, pw, psw, 0)
-    natural_start(nat.at[1], tf, pf, psf, 1)
-
-    zero = jnp.zeros((2, 128, 128), F32)
+    natural_prepare(nat.at[1], tf, psf)
+    start(copies0(tf, pf, psf, 1))
+
+    for t in range(NTILES):
+        for k in range(K):
+            pv[t, pl.ds(8 * k, 8), :] = jnp.full((8, 128), prior[k] * 2.0 ** tile_level[t], F32)
     for ref in (zs, qs, ss, ds, xs, us, ws):
-        ref[...] = zero
+        ref[...] = jnp.zeros_like(ref)
     rest = jnp.zeros((4, 128), F32)
     for t in range(2):
         for c in range(K):
@@ -279,7 +330,7 @@
     def weight(t, j):
         return jnp.where(mask[t] > 0.0, wt[t, pl.ds(pl.multiple_of(8 * j, 8), 8), :], 0.0)
 
-    def invert(t):
+    def invert(t, fine):
         w = [weight(t, j) for j in range(K)]
         for k in range(K):
             total = (dv[0, k] * w[0]) * dv[0, : k + 1]
@@ -287,10 +338,7 @@
                 total = total + (dv[j, k] * w[j]) * dv[j, : k + 1]
             a[k, : k + 1] = total
             a[k, k] = a[k, k] + 4.0 * pv[t, pl.ds(8 * k, 8), :]
-
-        @pl.when(t < 2)
-        def _():
-            for k in range(K):
+            if fine:
                 mb[t, k, : k + 1] = a[k, : k + 1]
                 if k:
                     mb[t, :k, k] = a[k, :k]
@@ -330,20 +378,19 @@
             if i:
                 mi[t, :i, i] = value[:i]
 
-    def invert_tiles(first, stop):
+    def invert_tiles(first, stop, fine=False):
         def step(t, carry):
-            invert(t)
+            invert(t, fine)
             return carry
 
         lax.fori_loop(first, stop, step, 0)
 
     finish(copies0(tw, pw, psw, 0))
     load0(tw, pw, wt)
-    start1(wt, s1w, r1w, 0)
-    invert_tiles(0, 3)
-    finish(copies1(s1w, r1w, 0))
-    load1(r1w, wt)
-    start2(wt, s2w, r2w, 2)
+    start1(wt, s1w, ssw, r1w, rsw, 0)
+    invert_tiles(0, 3, True)
+    finish(copies0(tf, pf, psf, 1))
+    load0(tf, pf, fb)
 
     def product(matrix, t, src):
         total = matrix[t, 0] * src[t, pl.ds(0, 8), :]
@@ -408,24 +455,25 @@
                 v[t] = keep * v[t] + product(mi, t, rho)
             return carry
 
-        lax.fori_loop(0, count, step, 0)
+        for i in range(count):
+            step(i, 0)
 
     up_rows = jnp.where(sub < 6, sub // 2, 7)
     up3 = lane % 64 // 2
     up2 = lane // 2 + 64 * (sub % 2)
     up1 = lane // 2 + 32
-    beside_lane = jnp.where(offset < 0, (offset + 4) // 2 + 30, offset // 2 + 96)
-    up1_side = jnp.where((offset >= -4) & (offset < 4), beside_lane, 0)
+    up1_side = jnp.where(offset < 0, (offset + 32) // 2 + 16, offset // 2 + 96)
     sub_even = sub % 2 == 0
 
     def cycle(wait_first, wait_second, k):
+        parity = lax.rem(k, 2)
+        beside_now = rsf.at[parity]
         descend(0)
-        start1(rho, s1f, r1f, 1)
+        start1(rho, s1f, ssf, r1f, beside_now, 1 + parity)
         wait_first()
-        finish(copies1(s1f, r1f, 1))
-        load1(r1f, fb)
+        finish(copies1(s1f, ssf, r1f, beside_now, 1 + parity))
+        load1(r1f, beside_now, fb)
         descend(1)
-        parity = lax.rem(k, 2)
         start2(rho, s2f, r2f.at[parity], parity)
         wait_second()
         finish2(r2f.at[parity], parity)
@@ -528,8 +576,13 @@
     scal[3] = jnp.zeros((8, 128), F32)
 
     def trip(k, carry):
-        finish(copies0(tf, pf, psf, 1))
-        load0(tf, pf, fb)
+        @pl.when(k > 0)
+        def _():
+            finish(copies_again())
+            load_main(tf, fb)
+            for c in range(K):
+                fb[2, pl.ds(8 * c, 8), :] = th[pl.ds(c, 8, stride=16), :]
+
         before = lax.rem(k + 1, 2)
 
         def turn():
@@ -539,37 +592,36 @@
 
             @pl.when(k == 0)
             def _():
+                finish(copies1(s1w, ssw, r1w, rsw, 0))
+                load1(r1w, rsw, wt)
+                start2(wt, s2w, r2w, 2)
                 invert_tiles(3, 5)
+
+        def coarse():
+            @pl.when(k == 0)
+            def _():
                 finish2(r2w, 2)
                 load2(r2w, wt)
                 restrict3(wt, wt)
-
-        def coarse():
-            @pl.when(k == 0)
+                invert_tiles(5, 7)
+
+            @pl.when(k > 0)
             def _():
-                invert_tiles(5, 7)
+                sum_finish(before, jnp.where(k > 1, 1.0, 0.0))
 
         cycle(turn, coarse, k)
         stencil(0, v, lambda t, rows, n: n)
-        for t in range(2):
+        for t in range(3):
             d1[t] = product(mb, t, v) - rho[t]
 
-        @pl.when(k > 0)
-        def _():
-            sum_finish(before, jnp.where(k > 1, 1.0, 0.0))
-
-        def update(new, old, ref, sum_ref, t, rows):
-            turned = new + scal[1] * old
-            ref[t, rows, :] = turned
-            return turned
-
-        for t in range(2):
+        for t in range(3):
             for c in range(K):
                 rows = pl.ds(8 * c, 8)
                 z = d1[t, rows, :] + scal[1] * zs[t, rows, :]
                 zs[t, rows, :] = z
                 old = ws[t, rows, :]
-                ss[t, rows, :] = old + scal[1] * ss[t, rows, :]
+                if t < 2:
+                    ss[t, rows, :] = old + scal[1] * ss[t, rows, :]
                 ws[t, rows, :] = old - scal[0] * z
 
         @pl.when(k < ITERS - 1)
@@ -577,8 +629,8 @@
             for i in range(4):
                 tf[pl.ds(32 * i, 16), :] = ws[0, pl.ds(i, 16, stride=8), :]
                 tf[pl.ds(32 * i + 16, 16), :] = ws[1, pl.ds(i, 16, stride=8), :]
-            pack(lambda c: jnp.where(sub < 4, ws[0, pl.ds(8 * c, 8), :], sroll(ws[1, pl.ds(8 * c, 8), :], 4)), psf)
-            start(copies0(tf, pf, psf, 1))
+                th[pl.ds(16 * i, 16), :] = ws[2, pl.ds(i, 16, stride=8), :]
+            start(copies_again())
 
         for t in range(2):
             for c in range(K):
@@ -632,14 +684,15 @@
         scratch_shapes=[
             vmem(K, 8, 128), pltpu.SMEM((K, K), F32), pltpu.SMEM((K,), F32), counts, counts, counts, dma(6),
             vmem(K, K, 8, 128), vmem(*field), vmem(10, 8, 128), vmem(*pair), vmem(*field),
-            vmem(K, K, 8, 128), vmem(NTILES, K, K, 8, 128), vmem(2, K, K, 8, 128),
+            vmem(K, K, 8, 128), vmem(NTILES, K, K, 8, 128), vmem(3, K, K, 8, 128),
             *[vmem(*field) for _ in range(5)],
-            *[vmem(*pair) for _ in range(8)], vmem(4, 8, 128),
-            vmem(256, 128), vmem(256, 128), vmem(6, 8, 128), vmem(6, 8, 128), vmem(8, 128), vmem(8, 128),
-            vmem(64, 128), vmem(64, 128), vmem(48, 128), vmem(48, 128), vmem(16, 128), vmem(16, 128),
-            vmem(3, 128, 128), vmem(3, 128, 128), vmem(128, 128), vmem(2, 128, 128),
+            *[vmem(3 if i in (0, 7) else 2, 128, 128) for i in range(8)], vmem(4, 8, 128),
+            vmem(256, 128), vmem(256, 128), vmem(128, 128), vmem(6, 32, 128), vmem(6, 32, 128), vmem(32, 128), vmem(32, 128),
+            vmem(64, 128), vmem(64, 128), vmem(2, 32, 128), vmem(48, 128), vmem(48, 128), vmem(2, 32, 128), vmem(2, 32, 128),
+            vmem(16, 128), vmem(16, 128),
+            vmem(128, 128), vmem(128, 128), vmem(2, 64, 128), vmem(2, 2, 64, 128), vmem(128, 128), vmem(2, 128, 128),
             vmem(1, 128), vmem(2, GX, 1, 128), vmem(2, GY, 1, 128), vmem(1, 128), vmem(GX * GY, 1, 128),
-            dma(2, 8), dma(2, 8), dma(2, 8), dma(2, 8), dma(3), dma(3), dma(2), dma(2), dma(2), dma(2),
+            dma(3, 8), dma(3, 8), dma(3, 8), dma(3, 8), dma(3), dma(3), dma(2), dma(2), dma(2), dma(2),
             pltpu.SemaphoreType.DMA, pltpu.SemaphoreType.DMA,
         ],
         compiler_params=pltpu.CompilerParams(collective_id=0, has_side_effects=True, vmem_limit_bytes=48 << 20),

time: 95.1 us -> 86.5 us (0.910)
  Pallas kernels: 89.4 us -> 80.8 us
    pallas_call x1, Pallas kernels: 89.4 us -> 80.8 us  [local(): pl.pallas_call(body, out_shape=jax.ShapeDtypeStruct(beta.shape, F32), in_...]
where the time goes in v3:
time: 86.5 us; the launch traced here: 86.2 us
  Pallas kernels  80.8 us (93%)
  local copies, waits for them, and re-layouts  5.34 us (6%)
    pallas_call x1, Pallas kernels, local(): pl.pallas_call(body, out_shape=jax.ShapeDtypeStruct(beta.shape, F32), in_...  80.8 us
    unnamed x13, local copies, waits for them, and re-layouts  5.34 us

profile of v3, /device:TPU:1, one launch (start us, length us, event | category | flops | bytes accessed | tf_op | source)
XLA Modules:
  0.0 86.2 jit_solution(15778607456872043644)
XLA Ops:
  0.0 0.0 copy-start
  0.0 0.8 copy-done
  0.8 0.0 copy-start.1
  0.8 0.8 copy-done.1
  1.7 0.0 copy-start.2
  1.7 0.8 copy-done.2
  2.5 0.0 copy-start.3
  2.5 0.8 copy-done.3
  3.4 0.0 copy-start.4
  3.4 0.7 copy-done.4
  4.1 0.0 copy-start.5
  4.1 0.7 copy-done.5
  4.7 80.8 %shard_map.64 = f32[16,8,128]{2,1,0:T(8,128)S(1)} custom-call(f32[16,8,128]{2,1,0:T(8,128)S(1)} %copy-done, f32[16,16]{1,0:T(8,128)S(1)} %copy-done.4, f32[16]{0:T(128)S(1)} %copy-done.5, s32[16,8,128]{2,1,0:T(8,128)S(1)} %copy-done.1, s32[16,8,128]{2,1,0:T(8,128)S(1)} %copy-done.2, s32[16,8,128]{2,1,0:T(8,128)S(1)} %copy-done.3), custom_call_target="tpu_custom_call" | custom-call | tf_op jit(solution)/shard_map/pallas_call | solution.py:679
  85.6 0.6 copy.8
Async XLA Ops:
  0.0 0.8 copy-start
  0.8 0.8 copy-start.1
  1.7 0.8 copy-start.2
  2.5 0.8 copy-start.3
  3.4 0.7 copy-start.4
  4.1 0.7 copy-start.5
